TPU v7x, 512 devices: a whole 4x8x8 slice. The times are simulated.
512 devices in a mesh: region: 32 (over x, z), batch: 16 (over y, core).
Axes of the slice: x: 4, y: 8, z: 8, core: 2. Of those that a mesh axis runs over, the one named last changes fastest.
Arguments:
- basis_values: bfloat16 [128, 2, 4096, 512], P('region', None, 'batch'), may hold values from -6 to 6
- dens_tiles: bfloat16 [128, 512, 512], P('region', 'batch'), may hold values from -0.005859375 to 0.005859375
- region_tiles: int32 [128, 3], replicated, may hold values from 0 to 127, as said below
- point_counts: int32 [128, 16], P('region', 'batch'), may hold values from 64 to 256, as said below
- point_weights: float32 [128, 4096], P('region', 'batch'), may hold values from 0.0078125 to 0.03125
Outputs:
- xc_tiles: float32 [128, 512, 512], P('region', 'batch')
Inputs may be any that keep to these rules, and one draw needn't show every extreme that they name: `region_tiles`: tile t is stored on index t // 4 of region. Regions 4 * i to 4 * i + 3 lie on index i; among their 12 entries no owner index holds more than 1 and some owner holds exactly 1, on every index; the entries of one owner on one index are different tiles. `point_counts`: every region has at least one batch with all 256 points live.
All inputs are finite; a program needn't handle non-finite values.
Results may differ from a plain program's by a relative error of at most 0.004.
Values may be sent and summed in bfloat16 or wider, within the bound.
A program may use at most 64 MiB of HBM per device.

v0:
```python
import jax
import jax.numpy as jnp
from jax import lax
from jax.sharding import PartitionSpec as P

SLATER = 0.9847450218426964


def potential(density):
    return -SLATER * density * jnp.power(density * density + 1.0, -1.0 / 3.0)


def shards(basis_values, dens_tiles, region_tiles, point_counts, point_weights):
    owner_count = lax.axis_size("region")
    batch_count = lax.axis_size("batch")
    my_index = lax.axis_index("region")
    region_local = basis_values.shape[0]
    point_local = basis_values.shape[2]
    tile_local = dens_tiles.shape[0]
    row_count = dens_tiles.shape[1]
    block_width = dens_tiles.shape[2]
    requests = 3 * region_local
    slot_total = (requests + owner_count - 1) // owner_count
    table = region_tiles.reshape(owner_count, requests)
    owners = table // tile_local
    local_ids = table % tile_local
    order = jnp.arange(requests, dtype=jnp.int32)
    earlier = (owners[:, :, None] == owners[:, None, :]) & (
        order[None, None, :] < order[None, :, None]
    )
    ranks = jnp.sum(earlier.astype(jnp.int32), axis=2)
    slot_ids = jnp.arange(slot_total, dtype=jnp.int32)
    tile_ids = jnp.arange(tile_local, dtype=jnp.int32)
    chosen = (
        (owners == my_index)[:, :, None, None]
        & (ranks[:, :, None, None] == slot_ids[None, None, :, None])
        & (local_ids[:, :, None, None] == tile_ids[None, None, None, :])
    )
    selector = jnp.sum(chosen.astype(jnp.float32), axis=1)
    my_owners = lax.dynamic_index_in_dim(owners, my_index, 0, keepdims=False)
    my_ranks = lax.dynamic_index_in_dim(ranks, my_index, 0, keepdims=False)
    outgoing = jnp.einsum(
        "dct,trb->dcrb",
        selector.astype(jnp.bfloat16),
        dens_tiles,
        preferred_element_type=jnp.float32,
    ).astype(jnp.bfloat16)
    incoming = lax.all_to_all(outgoing, "region", split_axis=0, concat_axis=0, tiled=True)
    flat = incoming.reshape(owner_count * slot_total, row_count, block_width)
    fetched = jnp.take(flat, my_owners * slot_total + my_ranks, axis=0)
    piece = lax.all_gather(fetched, "batch", axis=1, tiled=True)
    count = piece.shape[1]
    shaped = piece.reshape(region_local, 3, count, block_width)
    left_aa = jnp.einsum(
        "rpc,rcb->rpb", basis_values[:, 0], shaped[:, 0], preferred_element_type=jnp.float32
    )
    left_ab = jnp.einsum(
        "rpc,rcb->rpb", basis_values[:, 0], shaped[:, 1], preferred_element_type=jnp.float32
    )
    left_bb = jnp.einsum(
        "rpc,rcb->rpb", basis_values[:, 1], shaped[:, 2], preferred_element_type=jnp.float32
    )
    left_aa, left_ab, left_bb = (left_aa, left_ab, left_bb)
    phi_a = basis_values[:, 0]
    phi_b = basis_values[:, 1]
    density = (
        jnp.sum(phi_a * left_aa, axis=-1)
        + 2.0 * jnp.sum(phi_b * left_ab, axis=-1)
        + jnp.sum(phi_b * left_bb, axis=-1)
    )
    live = jnp.arange(point_local, dtype=jnp.int32)[None, :] < point_counts
    scale = jnp.where(live, point_weights * potential(density), 0.0)
    scaled_a = (scale[:, :, None] * phi_a).astype(jnp.bfloat16)
    scaled_b = (scale[:, :, None] * phi_b).astype(jnp.bfloat16)
    first = jnp.einsum("rpc,rpb->crb", phi_a, scaled_a, preferred_element_type=jnp.float32)
    second = jnp.einsum("rpc,rpb->crb", phi_a, scaled_b, preferred_element_type=jnp.float32)
    third = jnp.einsum("rpc,rpb->crb", phi_b, scaled_b, preferred_element_type=jnp.float32)
    partial_pairs = jnp.stack([first, second, third], axis=2).reshape(
        block_width, requests, block_width
    )
    partial_pairs = partial_pairs.astype(jnp.bfloat16).reshape(
        batch_count, row_count, requests, block_width
    )
    received = lax.all_to_all(partial_pairs, "batch", split_axis=0, concat_axis=0, tiled=True)
    pairs = jnp.sum(received.astype(jnp.float32), axis=0)
    placement = (
        (my_owners[:, None, None] == jnp.arange(owner_count, dtype=jnp.int32)[None, :, None])
        & (my_ranks[:, None, None] == slot_ids[None, None, :])
    ).astype(jnp.float32)
    outgoing_sums = jnp.einsum("jdc,rjb->dcrb", placement, pairs, precision=lax.Precision.HIGHEST)
    returned = lax.all_to_all(outgoing_sums, "region", split_axis=0, concat_axis=0, tiled=True)
    return jnp.einsum("dct,dcrb->trb", selector, returned, precision=lax.Precision.HIGHEST)


def solution(mesh):
    return jax.shard_map(
        shards,
        mesh=mesh,
        in_specs=(
            P("region", None, "batch", None),
            P("region", "batch", None),
            P(),
            P("region", "batch"),
            P("region", "batch"),
        ),
        out_specs=P("region", "batch", None),
        check_vma=False,
    )
```

profile of v0, /device:TPU:1, one launch (start us, length us, event | category | flops | bytes accessed | tf_op | source)
XLA Modules:
  0.0 331.1 jit_solution(2894611914320594194)
XLA Ops:
  6.5 0.0 copy-start
  6.5 0.8 copy.81
  7.4 0.1 reshape.254
  7.4 0.1 copy.82
  7.6 0.1 convert_reduce_fusion.1
  7.7 0.0 copy-done
  7.7 0.5 fusion.14
  8.2 1.6 copy.88
  9.8 0.0 copy-start.1
  9.8 13.8 %all-to-all-start = ((bf16[32,1,32,512]{3,2,1,0:T(8,128)(2,1)}), bf16[32,1,32,512]{3,2,1,0:T(8,128)(2,1)S(1)}, u32[]{:S(2)}, u32[]{:S(2)}) async-start(bf16[32,1,32,512]{3,2,1,0:T(8,128)(2,1)} %copy.88), calls=%async_computation | async-start | bytes 2097152 | tf_op jit(solution)/shard_map/all_to_all | solution.py:48
  23.6 0.0 all-gather.2.cloned.1.call-start
  23.7 0.2 dynamic-slice_reduce_fusion
  24.0 24.3 %all-to-all-done = bf16[32,1,32,512]{3,2,1,0:T(8,128)(2,1)S(1)} async-done(((bf16[32,1,32,512]{3,2,1,0:T(8,128)(2,1)}), bf16[32,1,32,512]{3,2,1,0:T(8,128)(2,1)S(1)}, u32[]{:S(2)}, u32[]{:S(2)}) %all-to-all-start) | async-done | bytes 1048608 | tf_op jit(solution)/shard_map/all_to_all | solution.py:48
  48.3 1.4 gather_fusion
  49.6 1.9 broadcast_select_fusion
  51.5 0.0 all-gather.2.cloned.1.call-update
  51.5 49.9 %all-gather.2.cloned.1.call-done = bf16[12,512,512]{2,1,0:T(8,128)(2,1)} async-done(((bf16[12,32,512]{2,1,0:T(8,128)(2,1)}), bf16[12,512,512]{2,1,0:T(8,128)(2,1)}) %all-gather.2.cloned.1.call-update) | async-done | bytes 6291472 | tf_op jit(solution)/shard_map/all_gather | solution.py:51
  101.5 0.0 copy-done.1
  101.5 0.0 copy-start.4
  101.5 2.5 fusion.2
  104.0 0.9 copy-done.4
  104.9 0.8 fusion
  105.7 0.0 copy-start.2
  105.7 0.0 copy-start.3
  105.7 0.8 fusion.3
  106.5 0.0 copy-done.2
  106.5 0.0 copy-done.3
  106.5 0.1 multiply_select_fusion
  106.6 0.9 convert_bitcast_fusion.1
  107.5 0.9 convert_bitcast_fusion
  108.4 0.9 convert_bitcast_fusion.2
  109.4 0.8 pad_maximum_fusion
  110.2 0.4 copy.99
  110.6 1.1 copy.100
  111.8 145.4 %all_to_all.15 = bf16[16,32,12,512]{3,1,2,0:T(8,128)(2,1)S(1)} all-to-all(bf16[16,32,12,512]{3,1,2,0:T(8,128)(2,1)S(1)} %copy.100), channel_id=1, replica_groups=mesh['region'=32,'batch'=16] {'batch'}, dimensions={0} | all-to-all | bytes 12582912 | tf_op jit(solution)/shard_map/all_to_all | solution.py:84
  257.1 1.3 convert_reduce_fusion
  258.4 1.4 convolution_bitcast_fusion
  259.8 1.2 copy.103
  261.0 60.3 %all_to_all.16 = f32[32,1,32,512]{3,2,1,0:T(8,128)S(1)} all-to-all(f32[32,1,32,512]{3,2,1,0:T(8,128)S(1)} %copy.103), channel_id=1, replica_groups=mesh['region'=32,'batch'=16] {'region'}, dimensions={0} | all-to-all | bytes 4194304 | tf_op jit(solution)/shard_map/all_to_all | solution.py:91
  321.3 2.2 fusion.8
  323.5 0.8 copy.105
  (7 shorter events, 0.1 us)
Async XLA Ops:
  6.5 1.2 copy-start
  9.8 91.7 %copy-start.1 = (bf16[4,2,256,512]{3,2,1,0:T(8,128)(2,1)S(1)}, bf16[4,2,256,512]{3,2,1,0:T(8,128)(2,1)}, u32[]{:S(2)}) copy-start(bf16[4,2,256,512]{3,2,1,0:T(8,128)(2,1)} %param.5) | copy-start | bytes 6291460
  9.8 38.5 %all-to-all-start = ((bf16[32,1,32,512]{3,2,1,0:T(8,128)(2,1)}), bf16[32,1,32,512]{3,2,1,0:T(8,128)(2,1)S(1)}, u32[]{:S(2)}, u32[]{:S(2)}) async-start(bf16[32,1,32,512]{3,2,1,0:T(8,128)(2,1)} %copy.88), calls=%async_computation | async-start | bytes 2097152 | tf_op jit(solution)/shard_map/all_to_all | solution.py:48
  23.6 77.8 %all-gather.2.cloned.1.call-start = ((), (), s32[]{:S(2)}) async-start(), calls=%async_computation.3 | async-start | bytes 6684672 | tf_op jit(solution)/shard_map/all_gather | solution.py:51
  101.5 3.4 %copy-start.4 = (bf16[12,512,512]{2,1,0:T(8,128)(2,1)S(1)}, bf16[12,512,512]{2,1,0:T(8,128)(2,1)}, u32[]{:S(2)}) copy-start(bf16[12,512,512]{2,1,0:T(8,128)(2,1)} %all-gather.2.cloned.1.call-done) | copy-start | bytes 18874372
  105.7 0.8 copy-start.2
  105.7 0.8 copy-start.3
Sparse Core Ops, SparseCore 0:
  51.6 49.7 all-gather.1
where the time goes:
time: 331 us
  blocking collectives  206 us (62%)
  waiting for transfers between devices  74.3 us (22%)
  starting transfers between devices  13.9 us (4%)
  between operations  13.6 us (4%)
  matrix products  11 us (3%)
  local copies, waits for them, and re-layouts  8.33 us (3%)
  other arithmetic  4.43 us (1%)
    all_to_all x1, blocking collectives, shards(): lax.all_to_all(partial_pairs, 'batch', split_axis=0, concat_axis=0, tiled...  145 us
    all_to_all x1, blocking collectives, shards(): lax.all_to_all(outgoing_sums, 'region', split_axis=0, concat_axis=0, tile...  60.3 us
    all_gather x1, waiting for transfers between devices, shards(): piece = lax.all_gather(fetched, 'batch', axis=1, tiled=True)  49.9 us
    all_to_all x1, waiting for transfers between devices, shards(): lax.all_to_all(outgoing, 'region', split_axis=0, concat_axis=0, tiled=True)  24.3 us
    all_to_all x1, starting transfers between devices, shards(): lax.all_to_all(outgoing, 'region', split_axis=0, concat_axis=0, tiled=True)  13.8 us
  transfers between devices with their start and end apart: 2, of which 2 were waited for; matrix products, arithmetic and copies ran while one was open for 0% of the time, Pallas kernels for 0%

commit v1 on v0

--- a/solution.py
+++ b/solution.py
@@ -48,7 +48,10 @@
     incoming = lax.all_to_all(outgoing, "region", split_axis=0, concat_axis=0, tiled=True)
     flat = incoming.reshape(owner_count * slot_total, row_count, block_width)
     fetched = jnp.take(flat, my_owners * slot_total + my_ranks, axis=0)
-    piece = lax.all_gather(fetched, "batch", axis=1, tiled=True)
+    piece = jnp.concatenate(
+        lax.all_to_all(jnp.stack([fetched for _ in range(lax.axis_size("batch"))]), "batch", 0, 0),
+        axis=1,
+    )
     count = piece.shape[1]
     shaped = piece.reshape(region_local, 3, count, block_width)
     left_aa = jnp.einsum(

time: 331 us -> 411 us (1.24)
  blocking collectives: 206 us -> 352 us
  waiting for transfers between devices: 74.3 us -> 24.4 us
  between operations: 13.6 us -> 0.21 us
    all_to_all x0 -> x1, blocking collectives: none -> 153 us  [shards(): lax.all_to_all(jnp.stack([fetched for _ in range(lax.axis_size('batch'))]...]
    all_gather x1 -> x0, waiting for transfers between devices: 49.9 us -> none  [shards(): piece = lax.all_gather(fetched, 'batch', axis=1, tiled=True)]
    all_to_all x1, blocking collectives: 60.3 us -> 55.2 us  [shards(): lax.all_to_all(outgoing_sums, 'region', split_axis=0, concat_axis=0, tile...]
  transfers between devices with their start and end apart: 2 -> 1, of which waited for: 2 -> 1; matrix products, arithmetic and copies ran while one was open for 0% -> 0% of each run, Pallas kernels for 0% -> 0%
where the time goes in v1:
time: 411 us
  blocking collectives  352 us (86%)
  waiting for transfers between devices  24.4 us (6%)
  starting transfers between devices  13.7 us (3%)
  matrix products  9.29 us (2%)
  local copies, waits for them, and re-layouts  9.03 us (2%)
    all_to_all x1, blocking collectives, shards(): lax.all_to_all(jnp.stack([fetched for _ in range(lax.axis_size('batch'))]...  153 us
    all_to_all x1, blocking collectives, shards(): lax.all_to_all(partial_pairs, 'batch', split_axis=0, concat_axis=0, tiled...  144 us
    all_to_all x1, blocking collectives, shards(): lax.all_to_all(outgoing_sums, 'region', split_axis=0, concat_axis=0, tile...  55.2 us
    all_to_all x1, waiting for transfers between devices, shards(): lax.all_to_all(outgoing, 'region', split_axis=0, concat_axis=0, tiled=True)  24.4 us
    all_to_all x1, starting transfers between devices, shards(): lax.all_to_all(outgoing, 'region', split_axis=0, concat_axis=0, tiled=True)  13.7 us
  transfers between devices with their start and end apart: 1, of which 1 were waited for; matrix products, arithmetic and copies ran while one was open for 0% of the time, Pallas kernels for 0%

profile of v1, /device:TPU:1, one launch (start us, length us, event | category | flops | bytes accessed | tf_op | source)
XLA Modules:
  0.0 410.8 jit_solution(12873191094888985087)
XLA Ops:
  0.0 0.0 copy-start
  0.0 0.8 copy.81
  0.8 0.1 reshape.256
  0.9 0.1 copy.82
  1.0 0.1 convert_reduce_fusion.1
  1.2 0.0 copy-done
  1.2 0.5 fusion.14
  1.7 1.6 copy.88
  3.3 13.7 %all-to-all-start = ((bf16[32,1,32,512]{3,2,1,0:T(8,128)(2,1)}), bf16[32,1,32,512]{3,2,1,0:T(8,128)(2,1)S(1)}, u32[]{:S(2)}, u32[]{:S(2)}) async-start(bf16[32,1,32,512]{3,2,1,0:T(8,128)(2,1)} %copy.88), calls=%async_computation | async-start | bytes 2097152 | tf_op jit(solution)/shard_map/all_to_all | solution.py:48
  17.0 0.2 dynamic-slice_reduce_fusion
  17.2 24.4 %all-to-all-done = bf16[32,1,32,512]{3,2,1,0:T(8,128)(2,1)S(1)} async-done(((bf16[32,1,32,512]{3,2,1,0:T(8,128)(2,1)}), bf16[32,1,32,512]{3,2,1,0:T(8,128)(2,1)S(1)}, u32[]{:S(2)}, u32[]{:S(2)}) %all-to-all-start) | async-done | bytes 1048608 | tf_op jit(solution)/shard_map/all_to_all | solution.py:48
  41.6 0.6 gather_fusion
  42.2 0.1 broadcast_select_fusion
  42.3 0.8 stack.14
  43.1 152.8 %all_to_all.20 = bf16[16,12,32,512]{3,2,1,0:T(8,128)(2,1)S(1)} all-to-all(bf16[16,12,32,512]{3,2,1,0:T(8,128)(2,1)S(1)} %stack.14), channel_id=1, replica_groups=mesh['region'=32,'batch'=16] {'batch'}, dimensions={0} | all-to-all | bytes 12582912 | tf_op jit(solution)/shard_map/all_to_all | solution.py:52
  195.9 0.0 copy-start.1
  195.9 1.1 copy.89
  197.0 0.5 copy-done.1
  197.5 0.8 fusion.2
  198.3 0.8 fusion
  199.1 0.0 copy-start.2
  199.1 0.0 copy-start.3
  199.1 0.8 fusion.3
  199.9 0.0 copy-done.2
  199.9 0.0 copy-done.3
  199.9 0.1 multiply_select_fusion
  200.0 0.9 convert_bitcast_fusion.1
  200.9 0.9 convert_bitcast_fusion
  201.8 0.9 convert_bitcast_fusion.2
  202.8 0.8 pad_maximum_fusion
  203.6 0.4 copy.100
  204.0 1.1 copy.101
  205.2 143.6 %all_to_all.21 = bf16[16,32,12,512]{3,1,2,0:T(8,128)(2,1)S(1)} all-to-all(bf16[16,32,12,512]{3,1,2,0:T(8,128)(2,1)S(1)} %copy.101), channel_id=1, replica_groups=mesh['region'=32,'batch'=16] {'batch'}, dimensions={0} | all-to-all | bytes 12582912 | tf_op jit(solution)/shard_map/all_to_all | solution.py:87
  348.8 1.3 convert_reduce_fusion
  350.0 1.4 convolution_bitcast_fusion
  351.4 1.2 copy.104
  352.7 55.2 %all_to_all.22 = f32[32,1,32,512]{3,2,1,0:T(8,128)S(1)} all-to-all(f32[32,1,32,512]{3,2,1,0:T(8,128)S(1)} %copy.104), channel_id=1, replica_groups=mesh['region'=32,'batch'=16] {'region'}, dimensions={0} | all-to-all | bytes 4194304 | tf_op jit(solution)/shard_map/all_to_all | solution.py:94
  407.8 2.2 fusion.8
  410.1 0.8 copy.106
  (7 shorter events, 0.1 us)
Async XLA Ops:
  0.0 1.2 copy-start
  3.3 38.3 %all-to-all-start = ((bf16[32,1,32,512]{3,2,1,0:T(8,128)(2,1)}), bf16[32,1,32,512]{3,2,1,0:T(8,128)(2,1)S(1)}, u32[]{:S(2)}, u32[]{:S(2)}) async-start(bf16[32,1,32,512]{3,2,1,0:T(8,128)(2,1)} %copy.88), calls=%async_computation | async-start | bytes 2097152 | tf_op jit(solution)/shard_map/all_to_all | solution.py:48
  195.9 1.6 copy-start.1
  199.1 0.8 copy-start.2
  199.1 0.8 copy-start.3
